TPU v7x, 32 devices: a whole 2x2x4 slice. The times are simulated.
32 devices in a mesh: heads: 4 (over y, x), fsdp: 8 (over z, core).
Axes of the slice: x: 2, y: 2, z: 4, core: 2. Of those that a mesh axis runs over, the one named last changes fastest.
Arguments:
- inputs: bfloat16 [8, 3072, 1280], P('fsdp', 'heads'), may hold values from -6 to 6
- cotangent: bfloat16 [8, 3072, 1280], P('fsdp', 'heads'), may hold values from -6 to 6
- lengths: int32 [8, 3], P('fsdp'), may hold values from 1 to 1024, 1536 in all within a row
- adapter_ids: int32 [8, 4], P('fsdp'), may hold values from 0 to 7
- query_weight: bfloat16 [1280, 1280], P('fsdp'), may hold values from -0.15625 to 0.15625
- key_weight: bfloat16 [1280, 1280], P('fsdp'), may hold values from -0.15625 to 0.15625
- value_weight: bfloat16 [1280, 1280], P('fsdp'), may hold values from -0.15625 to 0.15625
- out_weight: bfloat16 [1280, 1280], P('fsdp'), may hold values from -1.25 to 1.25
- up_weight: bfloat16 [1280, 1280], P('fsdp'), may hold values from -0.15625 to 0.15625
- down_weight: bfloat16 [1280, 1280], P('fsdp'), may hold values from -0.15625 to 0.15625
- attn_gain: bfloat16 [1280], replicated, may hold values from 0.099609375 to 1.8984375
- mlp_gain: bfloat16 [1280], replicated, may hold values from 0.099609375 to 1.8984375
- query_scale: float32 [80], replicated, may hold values from 0.5 to 2
- adapter_in: bfloat16 [4, 8, 1280, 16], replicated, may hold values from -0.15625 to 0.15625
- adapter_out: bfloat16 [4, 8, 16, 1280], replicated, may hold values from -1.5 to 1.5
Outputs:
- outputs: bfloat16 [8, 3072, 1280], P('fsdp', 'heads')
- grad_inputs: float32 [8, 3072, 1280], P('fsdp', 'heads')
- grad_adapter_in: float32 [4, 8, 1280, 16], replicated
- grad_adapter_out: float32 [4, 8, 16, 1280], replicated
Inputs may be any that keep to these rules, and one draw needn't show every extreme that they name: In every group the 3 lengths sum to 1536, and the longest is 1024.
All inputs are finite; a program needn't handle non-finite values.
Results may differ from a plain program's by a relative error of at most 0.015.
The roundings to bfloat16 on the way count: a program that leaves them out, or rounds other values in their place, can miss the bound.
Values may be sent and summed in bfloat16 or wider, within the bound.
No kernel may reach another device: no remote copies, remote signals or barrier semaphores. Data moves between devices by JAX's collectives and lax.ppermute only.
A program may use at most 256 MiB of HBM per device.

v0:
```python
import jax
import jax.numpy as jnp
from jax import lax
from jax.sharding import PartitionSpec as P

D = 1280
HEADS = 16
HEAD_DIM = 80
RANK = 16
ADAPTERS = 8
CONTS = 3
CONT_LEN = 512
PROMPT_LEN = 1536
GROUP_TOK = 3072
EPSILON = 1e-06


def product(left, right):
    return jnp.dot(left, right, preferred_element_type=jnp.float32)


def contract_rows(left, right):
    return lax.dot_general(
        left, right, (((0,), (0,)), ((), ())), preferred_element_type=jnp.float32
    )


def contract_cols(left, right):
    return lax.dot_general(
        left, right, (((1,), (1,)), ((), ())), preferred_element_type=jnp.float32
    )


def normalize(values, gain_vec):
    scaling = lax.rsqrt(jnp.mean(values * values, axis=-1, keepdims=True) + EPSILON)
    return (values * scaling * gain_vec, scaling)


def normalize_back(values, scaling, gain_vec, upstream):
    weighted = gain_vec * upstream
    return scaling * weighted - values * scaling**3 * jnp.mean(
        values * weighted, axis=-1, keepdims=True
    )


def segment_of(length_row):
    places = jnp.arange(GROUP_TOK, dtype=jnp.int32)
    bounds = jnp.cumsum(length_row)
    passed = jnp.sum((places[:, None] - PROMPT_LEN >= bounds[None, :]).astype(jnp.int32), axis=1)
    return jnp.where(places < PROMPT_LEN, 0, 1 + passed)


def picker(segments, id_row):
    member = (segments[:, None] == jnp.arange(CONTS + 1, dtype=jnp.int32)[None, :]).astype(
        jnp.int32
    )
    token_ids = jnp.sum(member * id_row[None, :], axis=1)
    columns = jnp.arange(ADAPTERS * RANK, dtype=jnp.int32) // RANK
    return (token_ids[:, None] == columns[None, :]).astype(jnp.float32)


def adapter_forward(normed_low, flat_down, flat_up, chosen):
    inner_low = (product(normed_low, flat_down) * chosen).astype(jnp.bfloat16)
    return (inner_low, product(inner_low, flat_up))


def adapter_backward(normed_low, inner_low, upstream_low, flat_down, flat_up, chosen):
    grad_up = contract_rows(inner_low, upstream_low)
    spread = (contract_cols(upstream_low, flat_up) * chosen).astype(jnp.bfloat16)
    grad_down = contract_rows(normed_low, spread)
    return (grad_down, grad_up, contract_cols(spread, flat_down))


def block_masks(segments):
    places = jnp.arange(GROUP_TOK, dtype=jnp.int32)
    block_count = GROUP_TOK // CONT_LEN
    return (
        places,
        segments == 0,
        places.reshape(block_count, CONT_LEN),
        segments.reshape(block_count, CONT_LEN),
    )


def attend_forward(query_heads, key_heads, value_heads, segments):
    block_count = GROUP_TOK // CONT_LEN
    width_here = query_heads.shape[1]
    heads_here = width_here // HEAD_DIM
    key_split = key_heads.reshape(GROUP_TOK, heads_here, HEAD_DIM)
    value_split = value_heads.reshape(GROUP_TOK, heads_here, HEAD_DIM)
    places, prompt_col, row_place_blocks, row_segment_blocks = block_masks(segments)

    def one_block(pieces):
        query_block, row_places, row_segments = pieces
        scores = jnp.einsum(
            "qhd,khd->hqk", query_block, key_split, preferred_element_type=jnp.float32
        )
        allowed = (places[None, :] <= row_places[:, None]) & (
            prompt_col[None, :] | (segments[None, :] == row_segments[:, None])
        )
        scores = jnp.where(allowed[None], scores, -1e30)
        largest = jnp.max(scores, axis=-1, keepdims=True)
        exponent = jnp.exp(scores - largest)
        row_total = jnp.sum(exponent, axis=-1, keepdims=True)
        probability = (exponent / row_total).astype(jnp.bfloat16)
        mixture = jnp.einsum(
            "hqk,khd->qhd", probability, value_split, preferred_element_type=jnp.float32
        )
        return (
            mixture.reshape(CONT_LEN, width_here).astype(jnp.bfloat16),
            (largest + jnp.log(row_total))[..., 0],
        )

    query_blocks = query_heads.reshape(block_count, CONT_LEN, heads_here, HEAD_DIM)
    mixture, logsum = lax.map(one_block, (query_blocks, row_place_blocks, row_segment_blocks))
    return (mixture.reshape(GROUP_TOK, width_here), logsum)


def attend_backward(query_heads, key_heads, value_heads, grad_heads, logsum, segments):
    block_count = GROUP_TOK // CONT_LEN
    width_here = query_heads.shape[1]
    heads_here = width_here // HEAD_DIM
    key_split = key_heads.reshape(GROUP_TOK, heads_here, HEAD_DIM)
    value_split = value_heads.reshape(GROUP_TOK, heads_here, HEAD_DIM)
    places, prompt_col, row_place_blocks, row_segment_blocks = block_masks(segments)

    def one_block(carry, pieces):
        grad_key_sum, grad_value_sum = carry
        query_block, grad_block, logsum_block, row_places, row_segments = pieces
        scores = jnp.einsum(
            "qhd,khd->hqk", query_block, key_split, preferred_element_type=jnp.float32
        )
        allowed = (places[None, :] <= row_places[:, None]) & (
            prompt_col[None, :] | (segments[None, :] == row_segments[:, None])
        )
        scores = jnp.where(allowed[None], scores, -1e30)
        probability = jnp.exp(scores - logsum_block[..., None])
        upstream = jnp.einsum(
            "qhd,khd->hqk", grad_block, value_split, preferred_element_type=jnp.float32
        )
        centre = jnp.sum(upstream * probability, axis=-1, keepdims=True)
        grad_scores = (probability * (upstream - centre)).astype(jnp.bfloat16)
        grad_query = jnp.einsum(
            "hqk,khd->qhd", grad_scores, key_split, preferred_element_type=jnp.float32
        )
        grad_key_sum = grad_key_sum + jnp.einsum(
            "hqk,qhd->khd", grad_scores, query_block, preferred_element_type=jnp.float32
        )
        grad_value_sum = grad_value_sum + jnp.einsum(
            "hqk,qhd->khd",
            probability.astype(jnp.bfloat16),
            grad_block,
            preferred_element_type=jnp.float32,
        )
        return (
            (grad_key_sum, grad_value_sum),
            grad_query.reshape(CONT_LEN, width_here).astype(jnp.bfloat16),
        )

    query_blocks = query_heads.reshape(block_count, CONT_LEN, heads_here, HEAD_DIM)
    grad_blocks = grad_heads.reshape(block_count, CONT_LEN, heads_here, HEAD_DIM)
    zeros_start = jnp.zeros((GROUP_TOK, heads_here, HEAD_DIM), jnp.float32)
    (grad_key_sum, grad_value_sum), grad_queries = lax.scan(
        one_block,
        (zeros_start, zeros_start),
        (query_blocks, grad_blocks, logsum, row_place_blocks, row_segment_blocks),
    )
    return (
        grad_queries.reshape(GROUP_TOK, width_here),
        grad_key_sum.reshape(GROUP_TOK, width_here).astype(jnp.bfloat16),
        grad_value_sum.reshape(GROUP_TOK, width_here).astype(jnp.bfloat16),
    )


def body(
    inputs,
    cotangent,
    lengths,
    adapter_ids,
    query_weight,
    key_weight,
    value_weight,
    out_weight,
    up_weight,
    down_weight,
    attn_gain,
    mlp_gain,
    query_scale,
    adapter_in,
    adapter_out,
):
    row_count = inputs.shape[1]
    offset = lax.axis_index("heads") * row_count
    segments = segment_of(lengths[0])
    chosen = picker(lax.dynamic_slice_in_dim(segments, offset, row_count), adapter_ids[0])
    flat_down = jnp.transpose(adapter_in, (0, 2, 1, 3)).reshape(4, D, ADAPTERS * RANK)
    flat_up = adapter_out.reshape(4, ADAPTERS * RANK, D)
    gain_attn = attn_gain.astype(jnp.float32)
    gain_mlp = mlp_gain.astype(jnp.float32)
    scale_row = jnp.tile(query_scale, HEADS) * HEAD_DIM ** (-0.5)
    w_query, w_key, w_value, w_out, w_up, w_down = (
        lax.all_gather(query_weight, "fsdp", axis=0, tiled=True),
        lax.all_gather(key_weight, "fsdp", axis=0, tiled=True),
        lax.all_gather(value_weight, "fsdp", axis=0, tiled=True),
        lax.all_gather(out_weight, "fsdp", axis=0, tiled=True),
        lax.all_gather(up_weight, "fsdp", axis=0, tiled=True),
        lax.all_gather(down_weight, "fsdp", axis=0, tiled=True),
    )
    rows_in = inputs[0].astype(jnp.float32)
    normed, scaling_attn = normalize(rows_in, gain_attn)
    normed_low = normed.astype(jnp.bfloat16)
    inner_query, extra_query = adapter_forward(normed_low, flat_down[0], flat_up[0], chosen)
    inner_value, extra_value = adapter_forward(normed_low, flat_down[1], flat_up[1], chosen)
    query_send = ((product(normed_low, w_query) + extra_query) * scale_row).astype(jnp.bfloat16)
    key_send = product(normed_low, w_key).astype(jnp.bfloat16)
    value_send = (product(normed_low, w_value) + extra_value).astype(jnp.bfloat16)
    query_heads, key_heads, value_heads = (
        lax.all_to_all(query_send, "heads", split_axis=1, concat_axis=0, tiled=True),
        lax.all_to_all(key_send, "heads", split_axis=1, concat_axis=0, tiled=True),
        lax.all_to_all(value_send, "heads", split_axis=1, concat_axis=0, tiled=True),
    )
    mixture, logsum = attend_forward(query_heads, key_heads, value_heads, segments)
    mixed_rows = lax.all_to_all(mixture, "heads", split_axis=0, concat_axis=1, tiled=True)
    middle = rows_in + product(mixed_rows, w_out)
    normed_mlp, scaling_mlp = normalize(middle, gain_mlp)
    normed_mlp_low = normed_mlp.astype(jnp.bfloat16)
    inner_up, extra_up = adapter_forward(normed_mlp_low, flat_down[2], flat_up[2], chosen)
    before = product(normed_mlp_low, w_up) + extra_up
    sigmoid_gate = jax.nn.sigmoid(before)
    hidden_low = (before * sigmoid_gate).astype(jnp.bfloat16)
    inner_down, extra_down = adapter_forward(hidden_low, flat_down[3], flat_up[3], chosen)
    outputs = (middle + (product(hidden_low, w_down) + extra_down)).astype(jnp.bfloat16)
    w_query, w_key, w_value, w_out, w_up, w_down = (
        lax.all_gather(query_weight, "fsdp", axis=0, tiled=True),
        lax.all_gather(key_weight, "fsdp", axis=0, tiled=True),
        lax.all_gather(value_weight, "fsdp", axis=0, tiled=True),
        lax.all_gather(out_weight, "fsdp", axis=0, tiled=True),
        lax.all_gather(up_weight, "fsdp", axis=0, tiled=True),
        lax.all_gather(down_weight, "fsdp", axis=0, tiled=True),
    )
    upstream = cotangent[0].astype(jnp.float32)
    grad_after = cotangent[0]
    down_first, down_second, back_down = adapter_backward(
        hidden_low, inner_down, grad_after, flat_down[3], flat_up[3], chosen
    )
    grad_hidden = contract_cols(grad_after, w_down) + back_down
    grad_before = (grad_hidden * sigmoid_gate * (1.0 + before * (1.0 - sigmoid_gate))).astype(
        jnp.bfloat16
    )
    up_first, up_second, back_up = adapter_backward(
        normed_mlp_low, inner_up, grad_before, flat_down[2], flat_up[2], chosen
    )
    grad_normed_mlp = contract_cols(grad_before, w_up) + back_up
    grad_middle = upstream + normalize_back(middle, scaling_mlp, gain_mlp, grad_normed_mlp)
    grad_branch = grad_middle.astype(jnp.bfloat16)
    grad_mixed = contract_cols(grad_branch, w_out).astype(jnp.bfloat16)
    grad_heads = lax.all_to_all(grad_mixed, "heads", split_axis=1, concat_axis=0, tiled=True)
    grad_query_heads, grad_key_heads, grad_value_heads = attend_backward(
        query_heads, key_heads, value_heads, grad_heads, logsum, segments
    )
    grad_query_rows, grad_key_rows, grad_value_rows = (
        lax.all_to_all(grad_query_heads, "heads", split_axis=0, concat_axis=1, tiled=True),
        lax.all_to_all(grad_key_heads, "heads", split_axis=0, concat_axis=1, tiled=True),
        lax.all_to_all(grad_value_heads, "heads", split_axis=0, concat_axis=1, tiled=True),
    )
    grad_query_pre = (grad_query_rows.astype(jnp.float32) * scale_row).astype(jnp.bfloat16)
    query_first, query_second, back_query = adapter_backward(
        normed_low, inner_query, grad_query_pre, flat_down[0], flat_up[0], chosen
    )
    value_first, value_second, back_value = adapter_backward(
        normed_low, inner_value, grad_value_rows, flat_down[1], flat_up[1], chosen
    )
    grad_normed = (
        contract_cols(grad_query_pre, w_query)
        + contract_cols(grad_key_rows, w_key)
        + contract_cols(grad_value_rows, w_value)
        + back_query
        + back_value
    )
    grad_inputs = grad_middle + normalize_back(rows_in, scaling_attn, gain_attn, grad_normed)
    first_terms = jnp.stack([query_first, value_first, up_first, down_first])
    second_terms = jnp.stack([query_second, value_second, up_second, down_second])
    first_total, second_total = lax.psum((first_terms, second_terms), ("heads", "fsdp"))
    grad_first = jnp.transpose(first_total.reshape(4, D, ADAPTERS, RANK), (0, 2, 1, 3))
    grad_second = second_total.reshape(4, ADAPTERS, RANK, D)
    return (outputs[None], grad_inputs[None], grad_first, grad_second)


def solution(mesh):
    placed = (
        P("fsdp", "heads", None),
        P("fsdp", "heads", None),
        P("fsdp", None),
        P("fsdp", None),
        P("fsdp", None),
        P("fsdp", None),
        P("fsdp", None),
        P("fsdp", None),
        P("fsdp", None),
        P("fsdp", None),
        P(),
        P(),
        P(),
        P(),
        P(),
    )
    return jax.shard_map(
        body,
        mesh=mesh,
        in_specs=placed,
        out_specs=(P("fsdp", "heads", None), P("fsdp", "heads", None), P(), P()),
        check_vma=False,
    )
```

profile of v0, /device:TPU:0, one launch (start us, length us, event | category | flops | bytes accessed | tf_op | source)
XLA Modules:
  0.0 1301.6 jit_solution(6721409575038360464)
XLA Ops:
  15.9 35.8 %all-gather.9.cloned.1.call-done = bf16[1280,1280]{1,0:T(8,128)(2,1)} async-done(((bf16[160,1280]{1,0:T(8,128)(2,1)}), bf16[1280,1280]{1,0:T(8,128)(2,1)}) %all-gather.9.cloned.1.call-update) | async-done | bytes 3276816 | tf_op jit(solution)/shard_map/all_gather | solution.py:203
  68.4 23.2 %all-gather.11.cloned.1.call-done = bf16[1280,1280]{1,0:T(8,128)(2,1)} async-done(((bf16[160,1280]{1,0:T(8,128)(2,1)}), bf16[1280,1280]{1,0:T(8,128)(2,1)}) %all-gather.11.cloned.1.call-update) | async-done | bytes 3276816 | tf_op jit(solution)/shard_map/all_gather | solution.py:204
  107.6 23.8 %all-gather.7.cloned.1.call-done = bf16[1280,1280]{1,0:T(8,128)(2,1)} async-done(((bf16[160,1280]{1,0:T(8,128)(2,1)}), bf16[1280,1280]{1,0:T(8,128)(2,1)}) %all-gather.7.cloned.1.call-update) | async-done | bytes 3276816 | tf_op jit(solution)/shard_map/all_gather | solution.py:202
  182.5 230.1 %while.28 = (s32[]{:T(128)}, bf16[6,512,320]{1,2,0:T(8,128)(2,1)}, f32[6,4,512]{2,1,0:T(4,128)}, s32[6,512]{1,0:T(8,128)S(1)}, pred[3072]{0:T(1024)(128)(4,1)S(1...) while((s32[]{:T(128)}, bf16[6,512,320]{1,2,0:T(8,128)(2,1)}, ...), condition=%wide.region_7.8_spmd.clone, body=%wide.region_4.7_spmd.clone.sunk | while | flops 2076342272 | bytes 94989472 | solution.py:115
  184.9 11.7 select_reduce_fusion.3
  196.6 11.9 fusion.193
  235.2 11.9 fusion.193
  273.5 11.7 fusion.193
  311.7 11.7 fusion.193
  349.9 11.7 fusion.193
  435.4 13.2 %all-to-all-done.3 = bf16[4,768,320]{1,2,0:T(8,128)(2,1)} async-done(((bf16[4,768,320]{1,2,0:T(8,128)(2,1)}), bf16[4,768,320]{1,2,0:T(8,128)(2,1)}, u32[]{:S(2)}, u32[]{:S(2)}) %all-to-all-start.3) | async-done | bytes 1966112 | tf_op jit(solution)/shard_map/all_to_all | solution.py:223
  488.9 23.0 %all-to-all-done.4 = bf16[768,4,320]{0,2,1:T(8,128)(2,1)} async-done(((bf16[768,4,320]{0,2,1:T(8,128)(2,1)}), bf16[768,4,320]{0,2,1:T(8,128)(2,1)}, u32[]{:S(2)}, u32[]{:S(2)}) %all-to-all-start.4) | async-done | bytes 1966112 | tf_op jit(solution)/shard_map/all_to_all | solution.py:257
  526.7 526.7 %while.29 = (s32[]{:T(128)}, f32[3072,4,80]{0,2,1:T(8,128)}, f32[3072,4,80]{0,2,1:T(8,128)}, bf16[6,512,320]{1,2,0:T(8,128)(2,1)}, bf16[6,512,4,80]{1,3,2,0:T(8,...) while((s32[]{:T(128)}, f32[3072,4,80]{0,2,1:T(8,128)}, ...), condition=%wide.region_12.13_spmd.clone, body=%wide.region_10.12_spmd.clone.sunk | while | flops 5119047680 | bytes 219360688 | solution.py:163
  542.3 12.7 fusion.207
  555.0 17.6 %multiply_reduce_fusion.4 = (f32[4,512]{1,0:T(4,128)S(1)}, f32[4,512,3072]{2,1,0:T(8,128)}) fusion(f32[4,512,3072]{2,1,0:T(8,128)} %fusion.204, f32[4,512]{1,0:T(4,128)S(1)} %dynamic-slice_bitcast_fusion.2, pred[512,3072]{1,0:T(8,128)(4,1)S(1)} %fusion.205, bf16[3072,4,80]{0,2,1:T(8,128)(2,1)} %get-tuple-element.610, ...), kind=kOutput, calls=%fused_computation.20.clone.1 | convolution fusion | flops 1031796736 | bytes 54214660 | tf_op jit(solution)/shard_map/while/body/eval_jaxpr/qhd,khd->hqk/dot_general | solution.py:138
  572.6 21.8 %multiply_convert_fusion.8 = bf16[4,512,3072]{2,1,0:T(8,128)(2,1)} fusion(f32[4,512,3072]{2,1,0:T(8,128)} %get-tuple-element.533, f32[4,512,3072]{2,1,0:T(8,128)} %fusion.204, f32[4,512]{1,0:T(4,128)S(1)} %get-tuple-element.534, f32[4,512]{1,0:T(4,128)S(1)} %dynamic-slice_bitcast_fusion.2, pred[512,3072]{1,0:T(8,128)(4,1)S(1)} %fusion.205), kind=kLoop, calls=%fused_computation.19.clone.1 | loop fusion | flops 31457280 | bytes 64503808 | tf_op jit(solution)/shard_map/while/body/eval_jaxpr/convert_element_type | solution.py:142
  628.1 13.9 %fusion.207 = f32[3072,4,80]{0,2,1:T(8,128)} fusion(f32[4,512,3072]{2,1,0:T(8,128)} %fusion.204, f32[4,512]{1,0:T(4,128)S(1)} %dynamic-slice_bitcast_fusion.2, pred[512,3072]{1,0:T(8,128)(4,1)S(1)} %fusion.205, f32[3072,4,80]{0,2,1:T(8,128)} %get-tuple-element.585, pred[]{:T(512)S(6)} %compare.7, bf16[6,512,4,80]{1,3,2,0:T(8,128)(2,1)} %get-tuple-element.609, ...), kind=kOutput, calls=%fused_computation.32.clone.1 | convolution fusion | flops 1027473408 | bytes 34938884 | tf_op jit(solution)/shard_map/while/body/eval_jaxpr/hqk,qhd->khd/dot_general | solution.py:149
  642.0 17.6 %multiply_reduce_fusion.4 = (f32[4,512]{1,0:T(4,128)S(1)}, f32[4,512,3072]{2,1,0:T(8,128)}) fusion(f32[4,512,3072]{2,1,0:T(8,128)} %fusion.204, f32[4,512]{1,0:T(4,128)S(1)} %dynamic-slice_bitcast_fusion.2, pred[512,3072]{1,0:T(8,128)(4,1)S(1)} %fusion.205, bf16[3072,4,80]{0,2,1:T(8,128)(2,1)} %get-tuple-element.610, ...), kind=kOutput, calls=%fused_computation.20.clone.1 | convolution fusion | flops 1031796736 | bytes 54214660 | tf_op jit(solution)/shard_map/while/body/eval_jaxpr/qhd,khd->hqk/dot_general | solution.py:138
  659.6 21.8 %multiply_convert_fusion.8 = bf16[4,512,3072]{2,1,0:T(8,128)(2,1)} fusion(f32[4,512,3072]{2,1,0:T(8,128)} %get-tuple-element.533, f32[4,512,3072]{2,1,0:T(8,128)} %fusion.204, f32[4,512]{1,0:T(4,128)S(1)} %get-tuple-element.534, f32[4,512]{1,0:T(4,128)S(1)} %dynamic-slice_bitcast_fusion.2, pred[512,3072]{1,0:T(8,128)(4,1)S(1)} %fusion.205), kind=kLoop, calls=%fused_computation.19.clone.1 | loop fusion | flops 31457280 | bytes 64503808 | tf_op jit(solution)/shard_map/while/body/eval_jaxpr/convert_element_type | solution.py:142
  716.2 13.9 %fusion.207 = f32[3072,4,80]{0,2,1:T(8,128)} fusion(f32[4,512,3072]{2,1,0:T(8,128)} %fusion.204, f32[4,512]{1,0:T(4,128)S(1)} %dynamic-slice_bitcast_fusion.2, pred[512,3072]{1,0:T(8,128)(4,1)S(1)} %fusion.205, f32[3072,4,80]{0,2,1:T(8,128)} %get-tuple-element.585, pred[]{:T(512)S(6)} %compare.7, bf16[6,512,4,80]{1,3,2,0:T(8,128)(2,1)} %get-tuple-element.609, ...), kind=kOutput, calls=%fused_computation.32.clone.1 | convolution fusion | flops 1027473408 | bytes 34938884 | tf_op jit(solution)/shard_map/while/body/eval_jaxpr/hqk,qhd->khd/dot_general | solution.py:149
  730.0 17.6 %multiply_reduce_fusion.4 = (f32[4,512]{1,0:T(4,128)S(1)}, f32[4,512,3072]{2,1,0:T(8,128)}) fusion(f32[4,512,3072]{2,1,0:T(8,128)} %fusion.204, f32[4,512]{1,0:T(4,128)S(1)} %dynamic-slice_bitcast_fusion.2, pred[512,3072]{1,0:T(8,128)(4,1)S(1)} %fusion.205, bf16[3072,4,80]{0,2,1:T(8,128)(2,1)} %get-tuple-element.610, ...), kind=kOutput, calls=%fused_computation.20.clone.1 | convolution fusion | flops 1031796736 | bytes 54214660 | tf_op jit(solution)/shard_map/while/body/eval_jaxpr/qhd,khd->hqk/dot_general | solution.py:138
  747.6 21.8 %multiply_convert_fusion.8 = bf16[4,512,3072]{2,1,0:T(8,128)(2,1)} fusion(f32[4,512,3072]{2,1,0:T(8,128)} %get-tuple-element.533, f32[4,512,3072]{2,1,0:T(8,128)} %fusion.204, f32[4,512]{1,0:T(4,128)S(1)} %get-tuple-element.534, f32[4,512]{1,0:T(4,128)S(1)} %dynamic-slice_bitcast_fusion.2, pred[512,3072]{1,0:T(8,128)(4,1)S(1)} %fusion.205), kind=kLoop, calls=%fused_computation.19.clone.1 | loop fusion | flops 31457280 | bytes 64503808 | tf_op jit(solution)/shard_map/while/body/eval_jaxpr/convert_element_type | solution.py:142
  804.2 13.9 %fusion.207 = f32[3072,4,80]{0,2,1:T(8,128)} fusion(f32[4,512,3072]{2,1,0:T(8,128)} %fusion.204, f32[4,512]{1,0:T(4,128)S(1)} %dynamic-slice_bitcast_fusion.2, pred[512,3072]{1,0:T(8,128)(4,1)S(1)} %fusion.205, f32[3072,4,80]{0,2,1:T(8,128)} %get-tuple-element.585, pred[]{:T(512)S(6)} %compare.7, bf16[6,512,4,80]{1,3,2,0:T(8,128)(2,1)} %get-tuple-element.609, ...), kind=kOutput, calls=%fused_computation.32.clone.1 | convolution fusion | flops 1027473408 | bytes 34938884 | tf_op jit(solution)/shard_map/while/body/eval_jaxpr/hqk,qhd->khd/dot_general | solution.py:149
  818.1 17.6 %multiply_reduce_fusion.4 = (f32[4,512]{1,0:T(4,128)S(1)}, f32[4,512,3072]{2,1,0:T(8,128)}) fusion(f32[4,512,3072]{2,1,0:T(8,128)} %fusion.204, f32[4,512]{1,0:T(4,128)S(1)} %dynamic-slice_bitcast_fusion.2, pred[512,3072]{1,0:T(8,128)(4,1)S(1)} %fusion.205, bf16[3072,4,80]{0,2,1:T(8,128)(2,1)} %get-tuple-element.610, ...), kind=kOutput, calls=%fused_computation.20.clone.1 | convolution fusion | flops 1031796736 | bytes 54214660 | tf_op jit(solution)/shard_map/while/body/eval_jaxpr/qhd,khd->hqk/dot_general | solution.py:138
  835.7 21.8 %multiply_convert_fusion.8 = bf16[4,512,3072]{2,1,0:T(8,128)(2,1)} fusion(f32[4,512,3072]{2,1,0:T(8,128)} %get-tuple-element.533, f32[4,512,3072]{2,1,0:T(8,128)} %fusion.204, f32[4,512]{1,0:T(4,128)S(1)} %get-tuple-element.534, f32[4,512]{1,0:T(4,128)S(1)} %dynamic-slice_bitcast_fusion.2, pred[512,3072]{1,0:T(8,128)(4,1)S(1)} %fusion.205), kind=kLoop, calls=%fused_computation.19.clone.1 | loop fusion | flops 31457280 | bytes 64503808 | tf_op jit(solution)/shard_map/while/body/eval_jaxpr/convert_element_type | solution.py:142
  892.3 13.9 %fusion.207 = f32[3072,4,80]{0,2,1:T(8,128)} fusion(f32[4,512,3072]{2,1,0:T(8,128)} %fusion.204, f32[4,512]{1,0:T(4,128)S(1)} %dynamic-slice_bitcast_fusion.2, pred[512,3072]{1,0:T(8,128)(4,1)S(1)} %fusion.205, f32[3072,4,80]{0,2,1:T(8,128)} %get-tuple-element.585, pred[]{:T(512)S(6)} %compare.7, bf16[6,512,4,80]{1,3,2,0:T(8,128)(2,1)} %get-tuple-element.609, ...), kind=kOutput, calls=%fused_computation.32.clone.1 | convolution fusion | flops 1027473408 | bytes 34938884 | tf_op jit(solution)/shard_map/while/body/eval_jaxpr/hqk,qhd->khd/dot_general | solution.py:149
  906.2 17.6 %multiply_reduce_fusion.4 = (f32[4,512]{1,0:T(4,128)S(1)}, f32[4,512,3072]{2,1,0:T(8,128)}) fusion(f32[4,512,3072]{2,1,0:T(8,128)} %fusion.204, f32[4,512]{1,0:T(4,128)S(1)} %dynamic-slice_bitcast_fusion.2, pred[512,3072]{1,0:T(8,128)(4,1)S(1)} %fusion.205, bf16[3072,4,80]{0,2,1:T(8,128)(2,1)} %get-tuple-element.610, ...), kind=kOutput, calls=%fused_computation.20.clone.1 | convolution fusion | flops 1031796736 | bytes 54214660 | tf_op jit(solution)/shard_map/while/body/eval_jaxpr/qhd,khd->hqk/dot_general | solution.py:138
  923.8 21.8 %multiply_convert_fusion.8 = bf16[4,512,3072]{2,1,0:T(8,128)(2,1)} fusion(f32[4,512,3072]{2,1,0:T(8,128)} %get-tuple-element.533, f32[4,512,3072]{2,1,0:T(8,128)} %fusion.204, f32[4,512]{1,0:T(4,128)S(1)} %get-tuple-element.534, f32[4,512]{1,0:T(4,128)S(1)} %dynamic-slice_bitcast_fusion.2, pred[512,3072]{1,0:T(8,128)(4,1)S(1)} %fusion.205), kind=kLoop, calls=%fused_computation.19.clone.1 | loop fusion | flops 31457280 | bytes 64503808 | tf_op jit(solution)/shard_map/while/body/eval_jaxpr/convert_element_type | solution.py:142
  980.4 13.9 %fusion.207 = f32[3072,4,80]{0,2,1:T(8,128)} fusion(f32[4,512,3072]{2,1,0:T(8,128)} %fusion.204, f32[4,512]{1,0:T(4,128)S(1)} %dynamic-slice_bitcast_fusion.2, pred[512,3072]{1,0:T(8,128)(4,1)S(1)} %fusion.205, f32[3072,4,80]{0,2,1:T(8,128)} %get-tuple-element.585, pred[]{:T(512)S(6)} %compare.7, bf16[6,512,4,80]{1,3,2,0:T(8,128)(2,1)} %get-tuple-element.609, ...), kind=kOutput, calls=%fused_computation.32.clone.1 | convolution fusion | flops 1027473408 | bytes 34938884 | tf_op jit(solution)/shard_map/while/body/eval_jaxpr/hqk,qhd->khd/dot_general | solution.py:149
  994.2 17.6 %multiply_reduce_fusion.4 = (f32[4,512]{1,0:T(4,128)S(1)}, f32[4,512,3072]{2,1,0:T(8,128)}) fusion(f32[4,512,3072]{2,1,0:T(8,128)} %fusion.204, f32[4,512]{1,0:T(4,128)S(1)} %dynamic-slice_bitcast_fusion.2, pred[512,3072]{1,0:T(8,128)(4,1)S(1)} %fusion.205, bf16[3072,4,80]{0,2,1:T(8,128)(2,1)} %get-tuple-element.610, ...), kind=kOutput, calls=%fused_computation.20.clone.1 | convolution fusion | flops 1031796736 | bytes 54214660 | tf_op jit(solution)/shard_map/while/body/eval_jaxpr/qhd,khd->hqk/dot_general | solution.py:138
  1011.8 21.8 %multiply_convert_fusion.8 = bf16[4,512,3072]{2,1,0:T(8,128)(2,1)} fusion(f32[4,512,3072]{2,1,0:T(8,128)} %get-tuple-element.533, f32[4,512,3072]{2,1,0:T(8,128)} %fusion.204, f32[4,512]{1,0:T(4,128)S(1)} %get-tuple-element.534, f32[4,512]{1,0:T(4,128)S(1)} %dynamic-slice_bitcast_fusion.2, pred[512,3072]{1,0:T(8,128)(4,1)S(1)} %fusion.205), kind=kLoop, calls=%fused_computation.19.clone.1 | loop fusion | flops 31457280 | bytes 64503808 | tf_op jit(solution)/shard_map/while/body/eval_jaxpr/convert_element_type | solution.py:142
  1167.7 121.7 %all-reduce.3.cloned.1.call-done = (f32[4,8,1280,16]{2,3,1,0:T(8,128)}, f32[4,8,16,1280]{3,2,1,0:T(8,128)}) async-done(((f32[4,8,1280,16]{2,3,1,0:T(8,128)}, f32[4,8,16,1280]{3,2,1,0:T(8,128)}), (f32[4,8,1280,16]{2,3,1,0:T(8,128)}, f32[4,8,16,1280]{3,2,1,0:T(8,128)})) %all-reduce.3.cloned.1.call-update) | async-done | bytes 5242896 | tf_op jit(solution)/shard_map/psum | solution.py:283
  (475 shorter events, 654.6 us)
Async XLA Ops:
  7.2 44.5 %all-gather.9.cloned.1.call-start = ((), (), s32[]{:S(2)}) async-start(), calls=%async_computation.9 | async-start | bytes 3686400 | tf_op jit(solution)/shard_map/all_gather | solution.py:203
  7.9 83.6 %all-gather.11.cloned.1.call-start = ((), (), s32[]{:S(2)}) async-start(), calls=%async_computation.10 | async-start | bytes 3686400 | tf_op jit(solution)/shard_map/all_gather | solution.py:204
  8.7 122.8 %all-gather.7.cloned.1.call-start = ((), (), s32[]{:S(2)}) async-start(), calls=%async_computation.8 | async-start | bytes 3686400 | tf_op jit(solution)/shard_map/all_gather | solution.py:202
  9.4 418.7 %all-gather.17.cloned.1.call-start = ((), (), s32[]{:S(2)}) async-start(), calls=%async_computation.13 | async-start | bytes 3686400 | tf_op jit(solution)/shard_map/all_gather | solution.py:207
  10.0 425.4 %all-gather.13.cloned.1.call-start = ((), (), s32[]{:S(2)}) async-start(), calls=%async_computation.11 | async-start | bytes 3686400 | tf_op jit(solution)/shard_map/all_gather | solution.py:205
  12.5 118.9 %copy-start.68 = (f32[768]{0:T(1024)}, f32[768]{0:T(1024)S(1)}, u32[]{:S(2)}) copy-start(f32[768]{0:T(1024)S(1)} %get-tuple-element.366) | copy-start | bytes 9220
  12.5 118.9 %copy-start.65 = (f32[1280]{0:T(1024)}, f32[1280]{0:T(1024)S(1)}, u32[]{:S(2)}) copy-start(f32[1280]{0:T(1024)S(1)} %convert_element_type.166) | copy-start | bytes 15364
  12.8 94.0 %copy-start.76 = (s32[768]{0:T(1024)}, s32[768]{0:T(1024)S(1)}, u32[]{:S(2)}) copy-start(s32[768]{0:T(1024)S(1)} %select_reduce_fusion.1) | copy-start | bytes 9220
  12.8 94.0 %copy-start.85 = (s32[128]{0:T(128)}, s32[128]{0:T(128)S(1)}, u32[]{:S(2)}) copy-start(s32[128]{0:T(128)S(1)} %and_select_fusion) | copy-start | bytes 1540
  15.1 42.6 %copy-start.30 = (bf16[1,1280,8,16]{1,3,2,0:T(8,128)(2,1)}, bf16[1,1280,8,16]{1,3,2,0:T(8,128)(2,1)S(1)}, u32[]{:S(2)}) copy-start(bf16[1,1280,8,16]{1,3,2,0:T(8,128)(2,1)S(1)} %get-tuple-element.361) | copy-start | bytes 983044
  15.1 91.8 %copy-start.39 = (bf16[1,1280,8,16]{1,3,2,0:T(8,128)(2,1)}, bf16[1,1280,8,16]{1,3,2,0:T(8,128)(2,1)S(1)}, u32[]{:S(2)}) copy-start(bf16[1,1280,8,16]{1,3,2,0:T(8,128)(2,1)S(1)} %get-tuple-element.362) | copy-start | bytes 983044
  15.8 80.4 %copy-start.43 = (bf16[768,128]{1,0:T(8,128)(2,1)}, bf16[768,128]{1,0:T(8,128)(2,1)S(1)}, u32[]{:S(2)}) copy-start(bf16[768,128]{1,0:T(8,128)(2,1)S(1)} %fusion.79) | copy-start | bytes 589828
  61.7 40.6 %all-to-all-start.1 = ((bf16[768,4,320]{0,2,1:T(8,128)(2,1)}), bf16[768,4,320]{0,2,1:T(8,128)(2,1)}, u32[]{:S(2)}, u32[]{:S(2)}) async-start(bf16[768,4,320]{0,2,1:T(8,128)(2,1)} %bitcast.288), calls=%async_computation.1 | async-start | bytes 3932160 | tf_op jit(solution)/shard_map/all_to_all | solution.py:219
  68.4 27.9 %copy-start.34 = (bf16[1,8,16,1280]{3,2,1,0:T(8,128)(2,1)}, bf16[1,8,16,1280]{3,2,1,0:T(8,128)(2,1)S(1)}, u32[]{:S(2)}) copy-start(bf16[1,8,16,1280]{3,2,1,0:T(8,128)(2,1)S(1)} %get-tuple-element.356) | copy-start | bytes 983044
  68.4 67.8 %copy-start.32 = (bf16[1,8,16,1280]{3,2,1,0:T(8,128)(2,1)}, bf16[1,8,16,1280]{3,2,1,0:T(8,128)(2,1)S(1)}, u32[]{:S(2)}) copy-start(bf16[1,8,16,1280]{3,2,1,0:T(8,128)(2,1)S(1)} %get-tuple-element.357) | copy-start | bytes 983044
  102.3 36.8 %all-to-all-start.2 = ((bf16[768,4,320]{0,2,1:T(8,128)(2,1)}), bf16[768,4,320]{0,2,1:T(8,128)(2,1)}, u32[]{:S(2)}, u32[]{:S(2)}) async-start(bf16[768,4,320]{0,2,1:T(8,128)(2,1)} %bitcast.287), calls=%async_computation.2 | async-start | bytes 3932160 | tf_op jit(solution)/shard_map/all_to_all | solution.py:220
  106.7 29.4 %copy-start.79 = (f32[80]{0:T(128)}, f32[80]{0:T(128)S(1)}, u32[]{:S(2)}) copy-start(f32[80]{0:T(128)S(1)} %broadcast_multiply_fusion.2) | copy-start | bytes 964
  106.8 29.3 %copy-start.61 = (f32[1280]{0:T(1024)}, f32[1280]{0:T(1024)S(1)}, u32[]{:S(2)}) copy-start(f32[1280]{0:T(1024)S(1)} %mul.223) | copy-start | bytes 15364
  107.6 28.6 %copy-start.41 = (bf16[768,128]{1,0:T(8,128)(2,1)}, bf16[768,128]{1,0:T(8,128)(2,1)S(1)}, u32[]{:S(2)}) copy-start(bf16[768,128]{1,0:T(8,128)(2,1)S(1)} %fusion.78) | copy-start | bytes 589828
  139.1 28.6 %all-to-all-start = ((bf16[768,4,320]{0,2,1:T(8,128)(2,1)}), bf16[768,4,320]{0,2,1:T(8,128)(2,1)}, u32[]{:S(2)}, u32[]{:S(2)}) async-start(bf16[768,4,320]{0,2,1:T(8,128)(2,1)} %bitcast.8), calls=%async_computation | async-start | bytes 3932160 | tf_op jit(solution)/shard_map/all_to_all | solution.py:218
  143.6 315.5 %all-gather.15.cloned.1.call-start = ((), (), s32[]{:S(2)}) async-start(), calls=%async_computation.12 | async-start | bytes 3686400 | tf_op jit(solution)/shard_map/all_gather | solution.py:206
  420.9 27.7 %all-to-all-start.3 = ((bf16[4,768,320]{1,2,0:T(8,128)(2,1)}), bf16[4,768,320]{1,2,0:T(8,128)(2,1)}, u32[]{:S(2)}, u32[]{:S(2)}) async-start(bf16[4,768,320]{1,2,0:T(8,128)(2,1)} %copy.81), calls=%async_computation.3 | async-start | bytes 3932160 | tf_op jit(solution)/shard_map/all_to_all | solution.py:223
  428.1 38.8 %copy-start.53 = (bf16[768,128]{1,0:T(8,128)(2,1)}, bf16[768,128]{1,0:T(8,128)(2,1)S(1)}, u32[]{:S(2)}) copy-start(bf16[768,128]{1,0:T(8,128)(2,1)S(1)} %fusion.85) | copy-start | bytes 589828
  454.8 18.2 %copy-start.63 = (f32[768]{0:T(1024)}, f32[768]{0:T(1024)S(1)}, u32[]{:S(2)}) copy-start(f32[768]{0:T(1024)S(1)} %get-tuple-element.368) | copy-start | bytes 9220
  454.8 18.2 %copy-start.70 = (f32[768]{0:T(1024)}, f32[768]{0:T(1024)S(1)}, u32[]{:S(2)}) copy-start(f32[768]{0:T(1024)S(1)} %get-tuple-element.367) | copy-start | bytes 9220
  484.4 27.5 %all-to-all-start.4 = ((bf16[768,4,320]{0,2,1:T(8,128)(2,1)}), bf16[768,4,320]{0,2,1:T(8,128)(2,1)}, u32[]{:S(2)}, u32[]{:S(2)}) async-start(bf16[768,4,320]{0,2,1:T(8,128)(2,1)} %bitcast.289), calls=%async_computation.4 | async-start | bytes 3932160 | tf_op jit(solution)/shard_map/all_to_all | solution.py:257
  612.7 15.4 %copy-start.48 = (pred[3072]{0:T(1024)(128)(4,1)}, pred[3072]{0:T(1024)(128)(4,1)S(1)}, u32[]{:S(2)}) copy-start(pred[3072]{0:T(1024)(128)(4,1)S(1)} %get-tuple-element.604) | copy-start | bytes 9220 | tf_op jit(solution)/shard_map/while
  700.8 15.4 %copy-start.48 = (pred[3072]{0:T(1024)(128)(4,1)}, pred[3072]{0:T(1024)(128)(4,1)S(1)}, u32[]{:S(2)}) copy-start(pred[3072]{0:T(1024)(128)(4,1)S(1)} %get-tuple-element.604) | copy-start | bytes 9220 | tf_op jit(solution)/shard_map/while
  1061.4 27.6 %all-to-all-start.7 = ((bf16[4,768,320]{1,2,0:T(8,128)(2,1)}), bf16[4,768,320]{1,2,0:T(8,128)(2,1)}, u32[]{:S(2)}, u32[]{:S(2)}) async-start(bf16[4,768,320]{1,2,0:T(8,128)(2,1)} %copy.90), calls=%async_computation.7 | async-start | bytes 3932160 | tf_op jit(solution)/shard_map/all_to_all | solution.py:264
  1089.0 26.7 %all-to-all-start.5 = ((bf16[4,768,320]{1,2,0:T(8,128)(2,1)}), bf16[4,768,320]{1,2,0:T(8,128)(2,1)S(1)}, u32[]{:S(2)}, u32[]{:S(2)}) async-start(bf16[4,768,320]{1,2,0:T(8,128)(2,1)} %copy.87), calls=%async_computation.5 | async-start | bytes 3932160 | tf_op jit(solution)/shard_map/all_to_all | solution.py:262
  1117.0 36.9 %all-to-all-start.6 = ((bf16[4,768,320]{1,2,0:T(8,128)(2,1)}), bf16[4,768,320]{1,2,0:T(8,128)(2,1)}, u32[]{:S(2)}, u32[]{:S(2)}) async-start(bf16[4,768,320]{1,2,0:T(8,128)(2,1)} %copy.89), calls=%async_computation.6 | async-start | bytes 3932160 | tf_op jit(solution)/shard_map/all_to_all | solution.py:263
  1121.5 168.0 %all-reduce.3.cloned.1.call-start = ((), (), s32[]{:S(2)}) async-start(), calls=%async_computation.14 | async-start | bytes 10485760 | tf_op jit(solution)/shard_map/psum | solution.py:283
  (117 other events, 692.7 us)
Sparse Core Ops, SparseCore 0:
  9.6 42.0 all-gather.8
  53.3 38.1 all-gather.10
  93.2 38.1 all-gather.6
  132.9 38.1 all-gather.16
  172.6 38.1 all-gather.12
  212.4 38.1 all-gather.14
  1141.9 147.4 all-reduce.2
where the time goes:
time: 1310 us; the launch traced here: 1300 us
  matrix products  603 us (46%)
  waiting for transfers between devices  260 us (20%)
  other arithmetic  252 us (19%)
  local copies, waits for them, and re-layouts  133 us (10%)
  starting transfers between devices  35.6 us (3%)
  between operations  15.4 us (1%)
    dot_general x12, matrix products, one_block(): jnp.einsum('qhd,khd->hqk', query_block, key_split, preferred_element_type...  137 us
    convert_element_type x6, other arithmetic, one_block(): grad_scores = (probability * (upstream - centre)).astype(jnp.bfloat16)  131 us
    psum x1, waiting for transfers between devices, body(): lax.psum((first_terms, second_terms), ('heads', 'fsdp'))  122 us
    dot_general x6, matrix products, one_block(): jnp.einsum('qhd,khd->hqk', grad_block, value_split, preferred_element_typ...  106 us
    dot_general x6, matrix products, one_block(): jnp.einsum('hqk,qhd->khd', probability.astype(jnp.bfloat16), grad_block,...  82 us
    reduce_sum x6, other arithmetic, one_block(): row_total = jnp.sum(exponent, axis=-1, keepdims=True)  70.7 us
    dot_general x6, matrix products, one_block(): jnp.einsum('hqk,khd->qhd', probability, value_split, preferred_element_ty...  68.5 us
    dot_general x6, matrix products, one_block(): jnp.einsum('hqk,qhd->khd', grad_scores, query_block, preferred_element_ty...  59.4 us
  transfers between devices with their start and end apart: 15, of which 8 were waited for; matrix products, arithmetic and copies ran while one was open for 31% of the time, Pallas kernels for 0%

commit v1 on v0

--- a/solution.py
+++ b/solution.py
@@ -254,7 +254,12 @@
     grad_middle = upstream + normalize_back(middle, scaling_mlp, gain_mlp, grad_normed_mlp)
     grad_branch = grad_middle.astype(jnp.bfloat16)
     grad_mixed = contract_cols(grad_branch, w_out).astype(jnp.bfloat16)
-    grad_heads = lax.all_to_all(grad_mixed, "heads", split_axis=1, concat_axis=0, tiled=True)
+    grad_heads = jnp.concatenate(
+        lax.all_to_all(
+            jnp.stack(jnp.split(grad_mixed, lax.axis_size("heads"), axis=1)), "heads", 0, 0
+        ),
+        axis=0,
+    )
     grad_query_heads, grad_key_heads, grad_value_heads = attend_backward(
         query_heads, key_heads, value_heads, grad_heads, logsum, segments
     )

time: 1310 us -> 1310 us (level)
  no operation moved by 1% of the time
where the time goes in v1:
time: 1310 us; the launch traced here: 1300 us
  matrix products  603 us (46%)
  waiting for transfers between devices  261 us (20%)
  other arithmetic  254 us (19%)
  local copies, waits for them, and re-layouts  134 us (10%)
  starting transfers between devices  35.6 us (3%)
  between operations  15.5 us (1%)
    dot_general x12, matrix products, one_block(): jnp.einsum('qhd,khd->hqk', query_block, key_split, preferred_element_type...  138 us
    convert_element_type x6, other arithmetic, one_block(): grad_scores = (probability * (upstream - centre)).astype(jnp.bfloat16)  131 us
    psum x1, waiting for transfers between devices, body(): lax.psum((first_terms, second_terms), ('heads', 'fsdp'))  122 us
    dot_general x6, matrix products, one_block(): jnp.einsum('qhd,khd->hqk', grad_block, value_split, preferred_element_typ...  106 us
    dot_general x6, matrix products, one_block(): jnp.einsum('hqk,qhd->khd', probability.astype(jnp.bfloat16), grad_block,...  81.9 us
    reduce_sum x6, other arithmetic, one_block(): row_total = jnp.sum(exponent, axis=-1, keepdims=True)  70.7 us
    dot_general x6, matrix products, one_block(): jnp.einsum('hqk,khd->qhd', probability, value_split, preferred_element_ty...  68.5 us
    dot_general x6, matrix products, one_block(): jnp.einsum('hqk,qhd->khd', grad_scores, query_block, preferred_element_ty...  59.4 us
  transfers between devices with their start and end apart: 15, of which 8 were waited for; matrix products, arithmetic and copies ran while one was open for 31% of the time, Pallas kernels for 0%

profile of v1, /device:TPU:0, one launch (start us, length us, event | category | flops | bytes accessed | tf_op | source)
XLA Modules:
  0.0 1303.6 jit_solution(4335301740198018552)
XLA Ops:
  15.9 35.8 %all-gather.9.cloned.1.call-done = bf16[1280,1280]{1,0:T(8,128)(2,1)} async-done(((bf16[160,1280]{1,0:T(8,128)(2,1)}), bf16[1280,1280]{1,0:T(8,128)(2,1)}) %all-gather.9.cloned.1.call-update) | async-done | bytes 3276816 | tf_op jit(solution)/shard_map/all_gather | solution.py:203
  68.4 23.2 %all-gather.11.cloned.1.call-done = bf16[1280,1280]{1,0:T(8,128)(2,1)} async-done(((bf16[160,1280]{1,0:T(8,128)(2,1)}), bf16[1280,1280]{1,0:T(8,128)(2,1)}) %all-gather.11.cloned.1.call-update) | async-done | bytes 3276816 | tf_op jit(solution)/shard_map/all_gather | solution.py:204
  107.6 23.8 %all-gather.7.cloned.1.call-done = bf16[1280,1280]{1,0:T(8,128)(2,1)} async-done(((bf16[160,1280]{1,0:T(8,128)(2,1)}), bf16[1280,1280]{1,0:T(8,128)(2,1)}) %all-gather.7.cloned.1.call-update) | async-done | bytes 3276816 | tf_op jit(solution)/shard_map/all_gather | solution.py:202
  182.6 230.2 %while.28 = (s32[]{:T(128)}, bf16[6,512,320]{1,2,0:T(8,128)(2,1)}, f32[6,4,512]{2,1,0:T(4,128)}, s32[6,512]{1,0:T(8,128)S(1)}, pred[3072]{0:T(1024)(128)(4,1)S(1...) while((s32[]{:T(128)}, bf16[6,512,320]{1,2,0:T(8,128)(2,1)}, ...), condition=%wide.region_7.8_spmd.clone, body=%wide.region_4.7_spmd.clone.sunk | while | flops 2076342272 | bytes 94989472 | solution.py:115
  196.7 11.9 fusion.193
  235.2 11.9 fusion.193
  273.6 11.7 fusion.193
  311.8 11.7 fusion.193
  350.0 11.7 fusion.193
  388.3 11.7 fusion.193
  435.5 13.3 %all-to-all-done.3 = bf16[4,768,320]{1,2,0:T(8,128)(2,1)} async-done(((bf16[4,768,320]{1,2,0:T(8,128)(2,1)}), bf16[4,768,320]{1,2,0:T(8,128)(2,1)}, u32[]{:S(2)}, u32[]{:S(2)}) %all-to-all-start.3) | async-done | bytes 1966112 | tf_op jit(solution)/shard_map/all_to_all | solution.py:223
  490.8 23.0 %all-to-all-done.4 = bf16[4,768,320]{1,2,0:T(8,128)(2,1)} async-done(((bf16[4,768,320]{1,2,0:T(8,128)(2,1)}), bf16[4,768,320]{1,2,0:T(8,128)(2,1)}, u32[]{:S(2)}, u32[]{:S(2)}) %all-to-all-start.4) | async-done | bytes 1966112 | tf_op jit(solution)/shard_map/all_to_all | solution.py:258
  528.7 526.7 %while.29 = (s32[]{:T(128)}, f32[3072,4,80]{0,2,1:T(8,128)}, f32[3072,4,80]{0,2,1:T(8,128)}, bf16[6,512,320]{1,2,0:T(8,128)(2,1)}, bf16[6,512,4,80]{1,3,2,0:T(8,...) while((s32[]{:T(128)}, f32[3072,4,80]{0,2,1:T(8,128)}, ...), condition=%wide.region_12.13_spmd.clone, body=%wide.region_10.12_spmd.clone.sunk | while | flops 5119047680 | bytes 219360688 | solution.py:163
  544.3 12.7 fusion.207
  557.1 17.6 %multiply_reduce_fusion.4 = (f32[4,512]{1,0:T(4,128)S(1)}, f32[4,512,3072]{2,1,0:T(8,128)}) fusion(f32[4,512,3072]{2,1,0:T(8,128)} %fusion.204, f32[4,512]{1,0:T(4,128)S(1)} %dynamic-slice_bitcast_fusion.2, pred[512,3072]{1,0:T(8,128)(4,1)S(1)} %fusion.205, bf16[3072,4,80]{0,2,1:T(8,128)(2,1)} %get-tuple-element.627, ...), kind=kOutput, calls=%fused_computation.20.clone.1 | convolution fusion | flops 1031796736 | bytes 54214660 | tf_op jit(solution)/shard_map/while/body/eval_jaxpr/qhd,khd->hqk/dot_general | solution.py:138
  574.6 21.8 %multiply_convert_fusion.8 = bf16[4,512,3072]{2,1,0:T(8,128)(2,1)} fusion(f32[4,512,3072]{2,1,0:T(8,128)} %get-tuple-element.550, f32[4,512,3072]{2,1,0:T(8,128)} %fusion.204, f32[4,512]{1,0:T(4,128)S(1)} %get-tuple-element.551, f32[4,512]{1,0:T(4,128)S(1)} %dynamic-slice_bitcast_fusion.2, pred[512,3072]{1,0:T(8,128)(4,1)S(1)} %fusion.205), kind=kLoop, calls=%fused_computation.19.clone.1 | loop fusion | flops 31457280 | bytes 64503808 | tf_op jit(solution)/shard_map/while/body/eval_jaxpr/convert_element_type | solution.py:142
  630.1 13.8 %fusion.207 = f32[3072,4,80]{0,2,1:T(8,128)} fusion(f32[4,512,3072]{2,1,0:T(8,128)} %fusion.204, f32[4,512]{1,0:T(4,128)S(1)} %dynamic-slice_bitcast_fusion.2, pred[512,3072]{1,0:T(8,128)(4,1)S(1)} %fusion.205, f32[3072,4,80]{0,2,1:T(8,128)} %get-tuple-element.602, pred[]{:T(512)S(6)} %compare.7, bf16[6,512,4,80]{1,3,2,0:T(8,128)(2,1)} %get-tuple-element.626, ...), kind=kOutput, calls=%fused_computation.32.clone.1 | convolution fusion | flops 1027473408 | bytes 34938884 | tf_op jit(solution)/shard_map/while/body/eval_jaxpr/hqk,qhd->khd/dot_general | solution.py:149
  644.0 17.6 %multiply_reduce_fusion.4 = (f32[4,512]{1,0:T(4,128)S(1)}, f32[4,512,3072]{2,1,0:T(8,128)}) fusion(f32[4,512,3072]{2,1,0:T(8,128)} %fusion.204, f32[4,512]{1,0:T(4,128)S(1)} %dynamic-slice_bitcast_fusion.2, pred[512,3072]{1,0:T(8,128)(4,1)S(1)} %fusion.205, bf16[3072,4,80]{0,2,1:T(8,128)(2,1)} %get-tuple-element.627, ...), kind=kOutput, calls=%fused_computation.20.clone.1 | convolution fusion | flops 1031796736 | bytes 54214660 | tf_op jit(solution)/shard_map/while/body/eval_jaxpr/qhd,khd->hqk/dot_general | solution.py:138
  661.6 21.8 %multiply_convert_fusion.8 = bf16[4,512,3072]{2,1,0:T(8,128)(2,1)} fusion(f32[4,512,3072]{2,1,0:T(8,128)} %get-tuple-element.550, f32[4,512,3072]{2,1,0:T(8,128)} %fusion.204, f32[4,512]{1,0:T(4,128)S(1)} %get-tuple-element.551, f32[4,512]{1,0:T(4,128)S(1)} %dynamic-slice_bitcast_fusion.2, pred[512,3072]{1,0:T(8,128)(4,1)S(1)} %fusion.205), kind=kLoop, calls=%fused_computation.19.clone.1 | loop fusion | flops 31457280 | bytes 64503808 | tf_op jit(solution)/shard_map/while/body/eval_jaxpr/convert_element_type | solution.py:142
  718.2 13.8 %fusion.207 = f32[3072,4,80]{0,2,1:T(8,128)} fusion(f32[4,512,3072]{2,1,0:T(8,128)} %fusion.204, f32[4,512]{1,0:T(4,128)S(1)} %dynamic-slice_bitcast_fusion.2, pred[512,3072]{1,0:T(8,128)(4,1)S(1)} %fusion.205, f32[3072,4,80]{0,2,1:T(8,128)} %get-tuple-element.602, pred[]{:T(512)S(6)} %compare.7, bf16[6,512,4,80]{1,3,2,0:T(8,128)(2,1)} %get-tuple-element.626, ...), kind=kOutput, calls=%fused_computation.32.clone.1 | convolution fusion | flops 1027473408 | bytes 34938884 | tf_op jit(solution)/shard_map/while/body/eval_jaxpr/hqk,qhd->khd/dot_general | solution.py:149
  732.0 17.6 %multiply_reduce_fusion.4 = (f32[4,512]{1,0:T(4,128)S(1)}, f32[4,512,3072]{2,1,0:T(8,128)}) fusion(f32[4,512,3072]{2,1,0:T(8,128)} %fusion.204, f32[4,512]{1,0:T(4,128)S(1)} %dynamic-slice_bitcast_fusion.2, pred[512,3072]{1,0:T(8,128)(4,1)S(1)} %fusion.205, bf16[3072,4,80]{0,2,1:T(8,128)(2,1)} %get-tuple-element.627, ...), kind=kOutput, calls=%fused_computation.20.clone.1 | convolution fusion | flops 1031796736 | bytes 54214660 | tf_op jit(solution)/shard_map/while/body/eval_jaxpr/qhd,khd->hqk/dot_general | solution.py:138
  749.6 21.8 %multiply_convert_fusion.8 = bf16[4,512,3072]{2,1,0:T(8,128)(2,1)} fusion(f32[4,512,3072]{2,1,0:T(8,128)} %get-tuple-element.550, f32[4,512,3072]{2,1,0:T(8,128)} %fusion.204, f32[4,512]{1,0:T(4,128)S(1)} %get-tuple-element.551, f32[4,512]{1,0:T(4,128)S(1)} %dynamic-slice_bitcast_fusion.2, pred[512,3072]{1,0:T(8,128)(4,1)S(1)} %fusion.205), kind=kLoop, calls=%fused_computation.19.clone.1 | loop fusion | flops 31457280 | bytes 64503808 | tf_op jit(solution)/shard_map/while/body/eval_jaxpr/convert_element_type | solution.py:142
  806.2 13.8 %fusion.207 = f32[3072,4,80]{0,2,1:T(8,128)} fusion(f32[4,512,3072]{2,1,0:T(8,128)} %fusion.204, f32[4,512]{1,0:T(4,128)S(1)} %dynamic-slice_bitcast_fusion.2, pred[512,3072]{1,0:T(8,128)(4,1)S(1)} %fusion.205, f32[3072,4,80]{0,2,1:T(8,128)} %get-tuple-element.602, pred[]{:T(512)S(6)} %compare.7, bf16[6,512,4,80]{1,3,2,0:T(8,128)(2,1)} %get-tuple-element.626, ...), kind=kOutput, calls=%fused_computation.32.clone.1 | convolution fusion | flops 1027473408 | bytes 34938884 | tf_op jit(solution)/shard_map/while/body/eval_jaxpr/hqk,qhd->khd/dot_general | solution.py:149
  820.0 17.6 %multiply_reduce_fusion.4 = (f32[4,512]{1,0:T(4,128)S(1)}, f32[4,512,3072]{2,1,0:T(8,128)}) fusion(f32[4,512,3072]{2,1,0:T(8,128)} %fusion.204, f32[4,512]{1,0:T(4,128)S(1)} %dynamic-slice_bitcast_fusion.2, pred[512,3072]{1,0:T(8,128)(4,1)S(1)} %fusion.205, bf16[3072,4,80]{0,2,1:T(8,128)(2,1)} %get-tuple-element.627, ...), kind=kOutput, calls=%fused_computation.20.clone.1 | convolution fusion | flops 1031796736 | bytes 54214660 | tf_op jit(solution)/shard_map/while/body/eval_jaxpr/qhd,khd->hqk/dot_general | solution.py:138
  837.6 21.8 %multiply_convert_fusion.8 = bf16[4,512,3072]{2,1,0:T(8,128)(2,1)} fusion(f32[4,512,3072]{2,1,0:T(8,128)} %get-tuple-element.550, f32[4,512,3072]{2,1,0:T(8,128)} %fusion.204, f32[4,512]{1,0:T(4,128)S(1)} %get-tuple-element.551, f32[4,512]{1,0:T(4,128)S(1)} %dynamic-slice_bitcast_fusion.2, pred[512,3072]{1,0:T(8,128)(4,1)S(1)} %fusion.205), kind=kLoop, calls=%fused_computation.19.clone.1 | loop fusion | flops 31457280 | bytes 64503808 | tf_op jit(solution)/shard_map/while/body/eval_jaxpr/convert_element_type | solution.py:142
  894.2 13.8 %fusion.207 = f32[3072,4,80]{0,2,1:T(8,128)} fusion(f32[4,512,3072]{2,1,0:T(8,128)} %fusion.204, f32[4,512]{1,0:T(4,128)S(1)} %dynamic-slice_bitcast_fusion.2, pred[512,3072]{1,0:T(8,128)(4,1)S(1)} %fusion.205, f32[3072,4,80]{0,2,1:T(8,128)} %get-tuple-element.602, pred[]{:T(512)S(6)} %compare.7, bf16[6,512,4,80]{1,3,2,0:T(8,128)(2,1)} %get-tuple-element.626, ...), kind=kOutput, calls=%fused_computation.32.clone.1 | convolution fusion | flops 1027473408 | bytes 34938884 | tf_op jit(solution)/shard_map/while/body/eval_jaxpr/hqk,qhd->khd/dot_general | solution.py:149
  908.1 17.6 %multiply_reduce_fusion.4 = (f32[4,512]{1,0:T(4,128)S(1)}, f32[4,512,3072]{2,1,0:T(8,128)}) fusion(f32[4,512,3072]{2,1,0:T(8,128)} %fusion.204, f32[4,512]{1,0:T(4,128)S(1)} %dynamic-slice_bitcast_fusion.2, pred[512,3072]{1,0:T(8,128)(4,1)S(1)} %fusion.205, bf16[3072,4,80]{0,2,1:T(8,128)(2,1)} %get-tuple-element.627, ...), kind=kOutput, calls=%fused_computation.20.clone.1 | convolution fusion | flops 1031796736 | bytes 54214660 | tf_op jit(solution)/shard_map/while/body/eval_jaxpr/qhd,khd->hqk/dot_general | solution.py:138
  925.7 21.8 %multiply_convert_fusion.8 = bf16[4,512,3072]{2,1,0:T(8,128)(2,1)} fusion(f32[4,512,3072]{2,1,0:T(8,128)} %get-tuple-element.550, f32[4,512,3072]{2,1,0:T(8,128)} %fusion.204, f32[4,512]{1,0:T(4,128)S(1)} %get-tuple-element.551, f32[4,512]{1,0:T(4,128)S(1)} %dynamic-slice_bitcast_fusion.2, pred[512,3072]{1,0:T(8,128)(4,1)S(1)} %fusion.205), kind=kLoop, calls=%fused_computation.19.clone.1 | loop fusion | flops 31457280 | bytes 64503808 | tf_op jit(solution)/shard_map/while/body/eval_jaxpr/convert_element_type | solution.py:142
  982.3 13.8 %fusion.207 = f32[3072,4,80]{0,2,1:T(8,128)} fusion(f32[4,512,3072]{2,1,0:T(8,128)} %fusion.204, f32[4,512]{1,0:T(4,128)S(1)} %dynamic-slice_bitcast_fusion.2, pred[512,3072]{1,0:T(8,128)(4,1)S(1)} %fusion.205, f32[3072,4,80]{0,2,1:T(8,128)} %get-tuple-element.602, pred[]{:T(512)S(6)} %compare.7, bf16[6,512,4,80]{1,3,2,0:T(8,128)(2,1)} %get-tuple-element.626, ...), kind=kOutput, calls=%fused_computation.32.clone.1 | convolution fusion | flops 1027473408 | bytes 34938884 | tf_op jit(solution)/shard_map/while/body/eval_jaxpr/hqk,qhd->khd/dot_general | solution.py:149
  996.1 17.6 %multiply_reduce_fusion.4 = (f32[4,512]{1,0:T(4,128)S(1)}, f32[4,512,3072]{2,1,0:T(8,128)}) fusion(f32[4,512,3072]{2,1,0:T(8,128)} %fusion.204, f32[4,512]{1,0:T(4,128)S(1)} %dynamic-slice_bitcast_fusion.2, pred[512,3072]{1,0:T(8,128)(4,1)S(1)} %fusion.205, bf16[3072,4,80]{0,2,1:T(8,128)(2,1)} %get-tuple-element.627, ...), kind=kOutput, calls=%fused_computation.20.clone.1 | convolution fusion | flops 1031796736 | bytes 54214660 | tf_op jit(solution)/shard_map/while/body/eval_jaxpr/qhd,khd->hqk/dot_general | solution.py:138
  1013.7 21.8 %multiply_convert_fusion.8 = bf16[4,512,3072]{2,1,0:T(8,128)(2,1)} fusion(f32[4,512,3072]{2,1,0:T(8,128)} %get-tuple-element.550, f32[4,512,3072]{2,1,0:T(8,128)} %fusion.204, f32[4,512]{1,0:T(4,128)S(1)} %get-tuple-element.551, f32[4,512]{1,0:T(4,128)S(1)} %dynamic-slice_bitcast_fusion.2, pred[512,3072]{1,0:T(8,128)(4,1)S(1)} %fusion.205), kind=kLoop, calls=%fused_computation.19.clone.1 | loop fusion | flops 31457280 | bytes 64503808 | tf_op jit(solution)/shard_map/while/body/eval_jaxpr/convert_element_type | solution.py:142
  1169.6 121.9 %all-reduce.3.cloned.1.call-done = (f32[4,8,1280,16]{2,3,1,0:T(8,128)}, f32[4,8,16,1280]{3,2,1,0:T(8,128)}) async-done(((f32[4,8,1280,16]{2,3,1,0:T(8,128)}, f32[4,8,16,1280]{3,2,1,0:T(8,128)}), (f32[4,8,1280,16]{2,3,1,0:T(8,128)}, f32[4,8,16,1280]{3,2,1,0:T(8,128)})) %all-reduce.3.cloned.1.call-update) | async-done | bytes 5242896 | tf_op jit(solution)/shard_map/psum | solution.py:288
  (477 shorter events, 656.6 us)
Async XLA Ops:
  7.2 44.5 %all-gather.9.cloned.1.call-start = ((), (), s32[]{:S(2)}) async-start(), calls=%async_computation.9 | async-start | bytes 3686400 | tf_op jit(solution)/shard_map/all_gather | solution.py:203
  7.9 83.6 %all-gather.11.cloned.1.call-start = ((), (), s32[]{:S(2)}) async-start(), calls=%async_computation.10 | async-start | bytes 3686400 | tf_op jit(solution)/shard_map/all_gather | solution.py:204
  8.7 122.8 %all-gather.7.cloned.1.call-start = ((), (), s32[]{:S(2)}) async-start(), calls=%async_computation.8 | async-start | bytes 3686400 | tf_op jit(solution)/shard_map/all_gather | solution.py:202
  9.4 418.8 %all-gather.17.cloned.1.call-start = ((), (), s32[]{:S(2)}) async-start(), calls=%async_computation.13 | async-start | bytes 3686400 | tf_op jit(solution)/shard_map/all_gather | solution.py:207
  10.0 425.5 %all-gather.13.cloned.1.call-start = ((), (), s32[]{:S(2)}) async-start(), calls=%async_computation.11 | async-start | bytes 3686400 | tf_op jit(solution)/shard_map/all_gather | solution.py:205
  12.5 119.0 %copy-start.68 = (f32[768]{0:T(1024)}, f32[768]{0:T(1024)S(1)}, u32[]{:S(2)}) copy-start(f32[768]{0:T(1024)S(1)} %get-tuple-element.383) | copy-start | bytes 9220
  12.5 119.0 %copy-start.65 = (f32[1280]{0:T(1024)}, f32[1280]{0:T(1024)S(1)}, u32[]{:S(2)}) copy-start(f32[1280]{0:T(1024)S(1)} %convert_element_type.166) | copy-start | bytes 15364
  12.8 94.0 %copy-start.76 = (s32[768]{0:T(1024)}, s32[768]{0:T(1024)S(1)}, u32[]{:S(2)}) copy-start(s32[768]{0:T(1024)S(1)} %select_reduce_fusion.1) | copy-start | bytes 9220
  12.8 94.0 %copy-start.85 = (s32[128]{0:T(128)}, s32[128]{0:T(128)S(1)}, u32[]{:S(2)}) copy-start(s32[128]{0:T(128)S(1)} %and_select_fusion) | copy-start | bytes 1540
  15.1 42.6 %copy-start.30 = (bf16[1,1280,8,16]{1,3,2,0:T(8,128)(2,1)}, bf16[1,1280,8,16]{1,3,2,0:T(8,128)(2,1)S(1)}, u32[]{:S(2)}) copy-start(bf16[1,1280,8,16]{1,3,2,0:T(8,128)(2,1)S(1)} %get-tuple-element.378) | copy-start | bytes 983044
  15.1 91.7 %copy-start.39 = (bf16[1,1280,8,16]{1,3,2,0:T(8,128)(2,1)}, bf16[1,1280,8,16]{1,3,2,0:T(8,128)(2,1)S(1)}, u32[]{:S(2)}) copy-start(bf16[1,1280,8,16]{1,3,2,0:T(8,128)(2,1)S(1)} %get-tuple-element.379) | copy-start | bytes 983044
  15.9 80.4 %copy-start.43 = (bf16[768,128]{1,0:T(8,128)(2,1)}, bf16[768,128]{1,0:T(8,128)(2,1)S(1)}, u32[]{:S(2)}) copy-start(bf16[768,128]{1,0:T(8,128)(2,1)S(1)} %fusion.79) | copy-start | bytes 589828
  61.7 40.6 %all-to-all-start.1 = ((bf16[768,4,320]{0,2,1:T(8,128)(2,1)}), bf16[768,4,320]{0,2,1:T(8,128)(2,1)}, u32[]{:S(2)}, u32[]{:S(2)}) async-start(bf16[768,4,320]{0,2,1:T(8,128)(2,1)} %bitcast.294), calls=%async_computation.1 | async-start | bytes 3932160 | tf_op jit(solution)/shard_map/all_to_all | solution.py:219
  68.4 27.9 %copy-start.34 = (bf16[1,8,16,1280]{3,2,1,0:T(8,128)(2,1)}, bf16[1,8,16,1280]{3,2,1,0:T(8,128)(2,1)S(1)}, u32[]{:S(2)}) copy-start(bf16[1,8,16,1280]{3,2,1,0:T(8,128)(2,1)S(1)} %get-tuple-element.373) | copy-start | bytes 983044
  68.4 67.8 %copy-start.32 = (bf16[1,8,16,1280]{3,2,1,0:T(8,128)(2,1)}, bf16[1,8,16,1280]{3,2,1,0:T(8,128)(2,1)S(1)}, u32[]{:S(2)}) copy-start(bf16[1,8,16,1280]{3,2,1,0:T(8,128)(2,1)S(1)} %get-tuple-element.374) | copy-start | bytes 983044
  102.3 36.8 %all-to-all-start.2 = ((bf16[768,4,320]{0,2,1:T(8,128)(2,1)}), bf16[768,4,320]{0,2,1:T(8,128)(2,1)}, u32[]{:S(2)}, u32[]{:S(2)}) async-start(bf16[768,4,320]{0,2,1:T(8,128)(2,1)} %bitcast.293), calls=%async_computation.2 | async-start | bytes 3932160 | tf_op jit(solution)/shard_map/all_to_all | solution.py:220
  106.7 29.4 %copy-start.79 = (f32[80]{0:T(128)}, f32[80]{0:T(128)S(1)}, u32[]{:S(2)}) copy-start(f32[80]{0:T(128)S(1)} %broadcast_multiply_fusion.2) | copy-start | bytes 964
  106.8 29.3 %copy-start.61 = (f32[1280]{0:T(1024)}, f32[1280]{0:T(1024)S(1)}, u32[]{:S(2)}) copy-start(f32[1280]{0:T(1024)S(1)} %mul.223) | copy-start | bytes 15364
  107.6 28.6 %copy-start.41 = (bf16[768,128]{1,0:T(8,128)(2,1)}, bf16[768,128]{1,0:T(8,128)(2,1)S(1)}, u32[]{:S(2)}) copy-start(bf16[768,128]{1,0:T(8,128)(2,1)S(1)} %fusion.78) | copy-start | bytes 589828
  139.1 28.7 %all-to-all-start = ((bf16[768,4,320]{0,2,1:T(8,128)(2,1)}), bf16[768,4,320]{0,2,1:T(8,128)(2,1)}, u32[]{:S(2)}, u32[]{:S(2)}) async-start(bf16[768,4,320]{0,2,1:T(8,128)(2,1)} %bitcast.8), calls=%async_computation | async-start | bytes 3932160 | tf_op jit(solution)/shard_map/all_to_all | solution.py:218
  143.6 315.7 %all-gather.15.cloned.1.call-start = ((), (), s32[]{:S(2)}) async-start(), calls=%async_computation.12 | async-start | bytes 3686400 | tf_op jit(solution)/shard_map/all_gather | solution.py:206
  421.1 27.8 %all-to-all-start.3 = ((bf16[4,768,320]{1,2,0:T(8,128)(2,1)}), bf16[4,768,320]{1,2,0:T(8,128)(2,1)}, u32[]{:S(2)}, u32[]{:S(2)}) async-start(bf16[4,768,320]{1,2,0:T(8,128)(2,1)} %copy.80), calls=%async_computation.3 | async-start | bytes 3932160 | tf_op jit(solution)/shard_map/all_to_all | solution.py:223
  428.2 39.0 %copy-start.53 = (bf16[768,128]{1,0:T(8,128)(2,1)}, bf16[768,128]{1,0:T(8,128)(2,1)S(1)}, u32[]{:S(2)}) copy-start(bf16[768,128]{1,0:T(8,128)(2,1)S(1)} %fusion.85) | copy-start | bytes 589828
  455.0 18.4 %copy-start.63 = (f32[768]{0:T(1024)}, f32[768]{0:T(1024)S(1)}, u32[]{:S(2)}) copy-start(f32[768]{0:T(1024)S(1)} %get-tuple-element.385) | copy-start | bytes 9220
  455.0 18.4 %copy-start.70 = (f32[768]{0:T(1024)}, f32[768]{0:T(1024)S(1)}, u32[]{:S(2)}) copy-start(f32[768]{0:T(1024)S(1)} %get-tuple-element.384) | copy-start | bytes 9220
  486.4 27.5 %all-to-all-start.4 = ((bf16[4,768,320]{1,2,0:T(8,128)(2,1)}), bf16[4,768,320]{1,2,0:T(8,128)(2,1)}, u32[]{:S(2)}, u32[]{:S(2)}) async-start(bf16[4,768,320]{1,2,0:T(8,128)(2,1)} %copy.81), calls=%async_computation.4 | async-start | bytes 3932160 | tf_op jit(solution)/shard_map/all_to_all | solution.py:258
  702.7 15.4 %copy-start.48 = (pred[3072]{0:T(1024)(128)(4,1)}, pred[3072]{0:T(1024)(128)(4,1)S(1)}, u32[]{:S(2)}) copy-start(pred[3072]{0:T(1024)(128)(4,1)S(1)} %get-tuple-element.621) | copy-start | bytes 9220 | tf_op jit(solution)/shard_map/while
  790.8 15.4 %copy-start.48 = (pred[3072]{0:T(1024)(128)(4,1)}, pred[3072]{0:T(1024)(128)(4,1)S(1)}, u32[]{:S(2)}) copy-start(pred[3072]{0:T(1024)(128)(4,1)S(1)} %get-tuple-element.621) | copy-start | bytes 9220 | tf_op jit(solution)/shard_map/while
  1063.3 27.6 %all-to-all-start.7 = ((bf16[4,768,320]{1,2,0:T(8,128)(2,1)}), bf16[4,768,320]{1,2,0:T(8,128)(2,1)}, u32[]{:S(2)}, u32[]{:S(2)}) async-start(bf16[4,768,320]{1,2,0:T(8,128)(2,1)} %copy.89), calls=%async_computation.7 | async-start | bytes 3932160 | tf_op jit(solution)/shard_map/all_to_all | solution.py:269
  1090.9 26.7 %all-to-all-start.5 = ((bf16[4,768,320]{1,2,0:T(8,128)(2,1)}), bf16[4,768,320]{1,2,0:T(8,128)(2,1)S(1)}, u32[]{:S(2)}, u32[]{:S(2)}) async-start(bf16[4,768,320]{1,2,0:T(8,128)(2,1)} %copy.86), calls=%async_computation.5 | async-start | bytes 3932160 | tf_op jit(solution)/shard_map/all_to_all | solution.py:267
  1118.9 36.9 %all-to-all-start.6 = ((bf16[4,768,320]{1,2,0:T(8,128)(2,1)}), bf16[4,768,320]{1,2,0:T(8,128)(2,1)}, u32[]{:S(2)}, u32[]{:S(2)}) async-start(bf16[4,768,320]{1,2,0:T(8,128)(2,1)} %copy.88), calls=%async_computation.6 | async-start | bytes 3932160 | tf_op jit(solution)/shard_map/all_to_all | solution.py:268
  1123.4 168.1 %all-reduce.3.cloned.1.call-start = ((), (), s32[]{:S(2)}) async-start(), calls=%async_computation.14 | async-start | bytes 10485760 | tf_op jit(solution)/shard_map/psum | solution.py:288
  (117 other events, 694.7 us)
Sparse Core Ops, SparseCore 0:
  9.6 42.0 all-gather.8
  53.3 38.1 all-gather.10
  93.2 38.1 all-gather.6
  132.9 38.1 all-gather.16
  172.6 38.1 all-gather.12
  212.4 38.1 all-gather.14
  1143.8 147.6 all-reduce.2
